TPU v7x, 32 devices: a whole 2x2x4 slice. The times are simulated.
32 devices in a mesh: col: 4 (over y, x), row: 8 (over z, core).
Axes of the slice: x: 2, y: 2, z: 4, core: 2. Of those that a mesh axis runs over, the one named last changes fastest.
Arguments:
- velocity: bfloat16 [4, 524288], P(None, ('col', 'row')), may hold values from -6 to 6
- pair_struct: int32 [4096], P(('col', 'row')), may hold values from 0 to 63
- pair_panel: int32 [4096], P(('col', 'row')), may hold values from 0 to 127
- pair_count: int32 [32], P(('col', 'row')), may hold values from 32 to 128, as said below
- mortar_coef: bfloat16 [4096, 128, 128], P(('col', 'row')), may hold values from -0.0625 to 0.0625
- bem_matrix: bfloat16 [32768, 32768], P('row', 'col'), may hold values from -0.03125 to 0.03125
- self_term: float32 [32768], P('row'), may hold values from 0.5 to 2
Outputs:
- pressure: bfloat16 [4, 32768], P(None, 'row')
- load: float32 [4, 524288], P(None, ('col', 'row'))
Inputs may be any that keep to these rules, and one draw needn't show every extreme that they name: pair_struct numbers a structural block within the slot's own device. `pair_count`: some device has all its slots live.
All inputs are finite; a program needn't handle non-finite values.
Results may differ from a plain program's by a relative error of at most 0.005.
Values may be sent and summed in bfloat16 or wider, within the bound.
No kernel may reach another device: no remote copies, remote signals or barrier semaphores. Data moves between devices by JAX's collectives and lax.ppermute only.
A program may use at most 128 MiB of HBM per device.

v0:
```python
import jax
import jax.numpy as jnp
from jax import lax
from jax.sharding import PartitionSpec as P

PANELS = 16384


def split_parts(blocks):
    return jnp.stack([blocks[..., 0::2], blocks[..., 1::2]], axis=1)


def on_device(velocity, pair_struct, pair_panel, pair_count, mortar_coef, bem_matrix, self_term):
    cases = velocity.shape[0]
    slots = pair_struct.shape[0]
    block = mortar_coef.shape[1]
    node_blocks = velocity.shape[1] // (2 * block)
    panel_blocks = PANELS // block
    live_mask = jnp.arange(slots, dtype=jnp.int32) < pair_count[0]
    vel_blocks = velocity.reshape(cases, node_blocks, 2 * block)
    picked = split_parts(jnp.take(vel_blocks, pair_struct, axis=1))
    pair_terms = jnp.einsum(
        "qpn,ckqn->ckqp", mortar_coef, picked, preferred_element_type=jnp.float32
    )
    panel_onehot = (
        (pair_panel[:, None] == jnp.arange(panel_blocks, dtype=jnp.int32)[None, :])
        & live_mask[:, None]
    ).astype(jnp.float32)
    spread_parts = jnp.einsum(
        "qb,ckqp->ckbp", panel_onehot, pair_terms, precision=lax.Precision.HIGHEST
    )
    spread_sum = spread_parts.transpose(0, 2, 3, 1).reshape(cases, 2 * PANELS)
    width_col = 2 * PANELS // lax.axis_size("col")
    width_row = 2 * PANELS // lax.axis_size("row")
    whole_sum = lax.psum(spread_sum, ("col", "row"))
    columns = lax.dynamic_slice_in_dim(
        whole_sum, lax.axis_index("col") * width_col, width_col, 1
    ).astype(jnp.bfloat16)
    row_start = lax.axis_index("row") * width_row
    owner = row_start // width_col == lax.axis_index("col")
    own_part = lax.dynamic_slice_in_dim(columns, row_start % width_col, width_row, 1).astype(
        jnp.float32
    )
    partial_value = lax.dot_general(
        columns, bem_matrix, (((1,), (1,)), ((), ())), preferred_element_type=jnp.float32
    )
    partial_value = partial_value + jnp.where(owner, self_term[None, :] * own_part, 0.0)
    pressure = lax.psum(partial_value, "col").astype(jnp.bfloat16)
    full_pressure = lax.all_gather(pressure, "row", axis=1, tiled=True)
    panel_view = full_pressure.reshape(cases, panel_blocks, 2 * block)
    took = split_parts(jnp.take(panel_view, pair_panel, axis=1))
    back_terms = jnp.einsum("qpn,ckqp->ckqn", mortar_coef, took, preferred_element_type=jnp.float32)
    node_onehot = (
        (pair_struct[:, None] == jnp.arange(node_blocks, dtype=jnp.int32)[None, :])
        & live_mask[:, None]
    ).astype(jnp.float32)
    load_parts = jnp.einsum(
        "qs,ckqn->cksn", node_onehot, back_terms, precision=lax.Precision.HIGHEST
    )
    load = load_parts.transpose(0, 2, 3, 1).reshape(cases, 2 * node_blocks * block)
    return (pressure, load)


def solution(mesh):
    placed = (
        P(None, ("col", "row")),
        P(("col", "row")),
        P(("col", "row")),
        P(("col", "row")),
        P(("col", "row"), None, None),
        P("row", "col"),
        P("row"),
    )
    return jax.shard_map(
        on_device,
        mesh=mesh,
        in_specs=placed,
        out_specs=(P(None, "row"), P(None, ("col", "row"))),
        check_vma=False,
    )
```

profile of v0, /device:TPU:0, one launch (start us, length us, event | category | flops | bytes accessed | tf_op | source)
XLA Modules:
  0.0 174.2 jit_solution(17576854343563618886)
XLA Ops:
  0.7 0.9 copy-done
  1.5 0.7 compare_select_fusion.1
  2.2 0.8 gather_fusion
  3.0 0.7 compare_and_fusion.1
  3.7 0.2 select_bitcast_fusion.1
  3.9 5.7 %slice.13 = bf16[4,128,128]{2,0,1:T(4,128)(2,1)S(1)} slice(bf16[4,128,256]{2,0,1:T(4,128)(2,1)S(1)} %select_bitcast_fusion.1), slice={[0:4:1], [0:128:1], [1:256:2]} | slice | bytes 262144 | tf_op jit(solution)/shard_map/slice | solution.py:10
  9.7 5.7 %slice.12 = bf16[4,128,128]{2,0,1:T(4,128)(2,1)S(1)} slice(bf16[4,128,256]{2,0,1:T(4,128)(2,1)S(1)} %select_bitcast_fusion.1), slice={[0:4:1], [0:128:1], [0:256:2]} | slice | bytes 262144 | tf_op jit(solution)/shard_map/slice | solution.py:10
  15.4 4.4 %fusion.2 = f32[128,4,2,128]{3,1,2,0:T(4,128)S(1)} fusion(bf16[128,128,128]{2,1,0:T(8,128)(2,1)} %param.11, bf16[4,1,128,128]{3,0,2,1:T(4,128)(2,1)S(1)} %bitcast.47, bf16[4,1,128,128]{3,0,2,1:T(4,128)(2,1)S(1)} %bitcast.48), kind=kOutput, calls=%fused_computation.5 | convolution fusion | flops 33685504 | bytes 4980736 | tf_op jit(solution)/shard_map/qpn,ckqn->ckqp/dot_general | solution.py:22
  19.8 0.3 copy.16
  20.8 0.5 convolution_bitcast_fusion
  21.2 12.1 %copy.9 = f32[4,128,128,2]{0,3,2,1:T(2,128)} copy(f32[4,128,128,2]{1,2,3,0:T(8,128)S(1)} %convolution_bitcast_fusion) | data formatting | bytes 1048576 | tf_op jit(solution)/shard_map/transpose;qb,ckqp->ckbp/transpose | solution.py:32
  33.4 9.5 %copy.10 = f32[4,32768]{1,0:T(4,128)S(1)} copy(f32[4,32768]{0,1:T(8,128)} %bitcast.44) | data formatting | bytes 1048576 | tf_op jit(solution)/shard_map/reshape | solution.py:32
  42.9 47.2 %all-reduce.1 = bf16[4,32768]{1,0:T(4,128)(2,1)S(1)} all-reduce(f32[4,32768]{1,0:T(4,128)S(1)} %copy.10), channel_id=1, replica_groups=mesh['col'=4,'row'=8] {'col','row'}, use_global_device_ids=true, to_apply=%region_0.1 | all-reduce | flops 131072 | bytes 786432 | tf_op jit(solution)/shard_map/psum | solution.py:35
  90.2 25.4 %convolution_add_fusion = f32[4,4096]{1,0:T(4,128)S(1)} fusion(bf16[4,8192]{1,0:T(4,128)(2,1)S(1)} %dynamic-slice_convert_fusion, bf16[4096,8192]{1,0:T(8,128)(2,1)} %param.12, s32[]{:T(128)S(6)} %select_n.48, f32[4096]{0:T(1024)S(1)} %copy-done.2, pred[]{:T(512)S(6)} %eq.34), kind=kOutput, calls=%fused_computation.2 | convolution fusion | flops 268500992 | bytes 67289096 | tf_op jit(solution)/shard_map/dot_general | solution.py:44
  115.6 16.1 %psum.15 = bf16[4,4096]{1,0:T(4,128)(2,1)S(1)} all-reduce(f32[4,4096]{1,0:T(4,128)S(1)} %convolution_add_fusion), channel_id=1, replica_groups=mesh['col'=4,'row'=8] {'col'}, use_global_device_ids=true, to_apply=%region_1.2 | all-reduce | flops 16384 | bytes 98304 | tf_op jit(solution)/shard_map/psum | solution.py:48
  131.7 14.4 %all_gather.3 = bf16[4,32768]{1,0:T(4,128)(2,1)S(1)} all-gather(bf16[4,4096]{1,0:T(4,128)(2,1)S(1)} %psum.15), channel_id=1, replica_groups=mesh['col'=4,'row'=8] {'row'}, dimensions={1}, use_global_device_ids=true | all-gather | bytes 294912 | tf_op jit(solution)/shard_map/all_gather | solution.py:49
  146.1 0.8 gather_fusion.1
  146.9 0.2 select_bitcast_fusion
  147.2 5.7 %slice.15 = bf16[4,128,128]{2,0,1:T(4,128)(2,1)S(1)} slice(bf16[4,128,256]{2,0,1:T(4,128)(2,1)S(1)} %select_bitcast_fusion), slice={[0:4:1], [0:128:1], [1:256:2]} | slice | bytes 262144 | tf_op jit(solution)/shard_map/slice | solution.py:10
  152.9 5.7 %slice.14 = bf16[4,128,128]{2,0,1:T(4,128)(2,1)S(1)} slice(bf16[4,128,256]{2,0,1:T(4,128)(2,1)S(1)} %select_bitcast_fusion), slice={[0:4:1], [0:128:1], [0:256:2]} | slice | bytes 262144 | tf_op jit(solution)/shard_map/slice | solution.py:10
  158.6 3.4 %fusion = f32[128,4,2,128]{3,1,2,0:T(4,128)S(1)} fusion(bf16[128,128,128]{2,1,0:T(8,128)(2,1)} %param.11, bf16[4,1,128,128]{3,0,2,1:T(4,128)(2,1)S(1)} %bitcast.49, bf16[4,1,128,128]{3,0,2,1:T(4,128)(2,1)S(1)} %bitcast.50), kind=kOutput, calls=%fused_computation.3 | convolution fusion | flops 33685504 | bytes 4980736 | tf_op jit(solution)/shard_map/qpn,ckqp->ckqn/dot_general | solution.py:52
  162.0 0.4 convolution_bitcast_fusion.1
  162.4 5.9 %copy.12 = f32[4,64,128,2]{0,3,2,1:T(2,128)} copy(f32[4,64,128,2]{2,1,3,0:T(8,128)S(1)} %convolution_bitcast_fusion.1) | data formatting | bytes 524288 | tf_op jit(solution)/shard_map/transpose;qs,ckqn->cksn/transpose | solution.py:60
  168.3 5.9 %copy.13 = f32[4,16384]{1,0:T(4,128)} copy(f32[4,16384]{0,1:T(8,128)} %bitcast.45) | data formatting | bytes 524288
  (15 shorter events, 0.1 us)
Async XLA Ops:
  0.6 0.9 copy-start
  0.6 20.1 %copy-start.3 = (s32[128]{0:T(128)S(1)}, s32[128]{0:T(128)}, u32[]{:S(2)}) copy-start(s32[128]{0:T(128)} %param.9) | copy-start | bytes 1540
  33.4 56.8 %copy-start.2 = (f32[4096]{0:T(1024)S(1)}, f32[4096]{0:T(1024)}, u32[]{:S(2)}) copy-start(f32[4096]{0:T(1024)} %param.13) | copy-start | bytes 49156
  115.6 46.4 %copy-start.4 = (s32[128]{0:T(128)S(1)}, s32[128]{0:T(128)}, u32[]{:S(2)}) copy-start(s32[128]{0:T(128)} %param.8) | copy-start | bytes 1540
  131.7 36.6 %copy-start.1 = (bf16[4,4096]{1,0:T(4,128)(2,1)}, bf16[4,4096]{1,0:T(4,128)(2,1)S(1)}, u32[]{:S(2)}) copy-start(bf16[4,4096]{1,0:T(4,128)(2,1)S(1)} %psum.15) | copy-start | bytes 98308
where the time goes:
time: 175 us; the launch traced here: 174 us
  blocking collectives  77.7 us (44%)
  local copies, waits for them, and re-layouts  59.1 us (34%)
  matrix products  34.1 us (19%)
  other arithmetic  1.8 us (1%)
    psum x1, blocking collectives, on_device(): whole_sum = lax.psum(spread_sum, ('col', 'row'))  47.2 us
    dot_general x1, matrix products, on_device(): lax.dot_general(columns, bem_matrix, (((1,), (1,)), ((), ())), preferred_...  25.4 us
    slice x4, local copies, waits for them, and re-layouts, split_parts(): return jnp.stack([blocks[..., 0::2], blocks[..., 1::2]], axis=1)  22.9 us
    psum x1, blocking collectives, on_device(): pressure = lax.psum(partial_value, 'col').astype(jnp.bfloat16)  16.1 us
    all_gather x1, blocking collectives, on_device(): full_pressure = lax.all_gather(pressure, 'row', axis=1, tiled=True)  14.4 us
    transpose x1, local copies, waits for them, and re-layouts, on_device(): spread_sum = spread_parts.transpose(0, 2, 3, 1).reshape(cases, 2 * PANELS)  12.1 us
    reshape x1, local copies, waits for them, and re-layouts, on_device(): spread_sum = spread_parts.transpose(0, 2, 3, 1).reshape(cases, 2 * PANELS)  9.48 us
    unnamed x11, local copies, waits for them, and re-layouts  6.83 us

commit v1 on v0

--- a/solution.py
+++ b/solution.py
@@ -32,7 +32,8 @@
     spread_sum = spread_parts.transpose(0, 2, 3, 1).reshape(cases, 2 * PANELS)
     width_col = 2 * PANELS // lax.axis_size("col")
     width_row = 2 * PANELS // lax.axis_size("row")
-    whole_sum = lax.psum(spread_sum, ("col", "row"))
+    parts = lax.all_gather(spread_sum, ("col", "row"), axis=0, tiled=False)
+    whole_sum = parts.sum(axis=0)
     columns = lax.dynamic_slice_in_dim(
         whole_sum, lax.axis_index("col") * width_col, width_col, 1
     ).astype(jnp.bfloat16)

time: 175 us -> 267 us (1.53)
  waiting for transfers between devices: 0 us -> 117 us
  blocking collectives: 77.7 us -> 30.3 us
  between operations: 1.5 us -> 14.9 us
  other arithmetic: 1.8 us -> 10.6 us
    all_gather x0 -> x1, waiting for transfers between devices: none -> 117 us  [on_device(): parts = lax.all_gather(spread_sum, ('col', 'row'), axis=0, tiled=False)]
    psum x1 -> x0, blocking collectives: 47.2 us -> none  [on_device(): whole_sum = lax.psum(spread_sum, ('col', 'row'))]
    another operation x0 -> x1, local copies, waits for them, and re-layouts: none -> 9.83 us  [on_device(): parts = lax.all_gather(spread_sum, ('col', 'row'), axis=0, tiled=False)]
    reshape x1 -> x0, local copies, waits for them, and re-layouts: 9.48 us -> none  [on_device(): spread_sum = spread_parts.transpose(0, 2, 3, 1).reshape(cases, 2 * PANELS)]
    reduce_sum x0 -> x1, other arithmetic: none -> 8.79 us  [on_device(): whole_sum = parts.sum(axis=0)]
  transfers between devices with their start and end apart: 0 -> 1, of which waited for: 0 -> 1; matrix products, arithmetic and copies ran while one was open for 0% -> 0% of each run, Pallas kernels for 0% -> 0%
where the time goes in v1:
time: 267 us; the launch traced here: 266 us
  waiting for transfers between devices  117 us (44%)
  local copies, waits for them, and re-layouts  58.3 us (22%)
  matrix products  35 us (13%)
  blocking collectives  30.3 us (11%)
  between operations  14.9 us (6%)
  other arithmetic  10.6 us (4%)
    all_gather x1, waiting for transfers between devices, on_device(): parts = lax.all_gather(spread_sum, ('col', 'row'), axis=0, tiled=False)  117 us
    dot_general x1, matrix products, on_device(): lax.dot_general(columns, bem_matrix, (((1,), (1,)), ((), ())), preferred_...  25.4 us
    slice x4, local copies, waits for them, and re-layouts, split_parts(): return jnp.stack([blocks[..., 0::2], blocks[..., 1::2]], axis=1)  22.9 us
    psum x1, blocking collectives, on_device(): pressure = lax.psum(partial_value, 'col').astype(jnp.bfloat16)  15.9 us
    all_gather x1, blocking collectives, on_device(): full_pressure = lax.all_gather(pressure, 'row', axis=1, tiled=True)  14.4 us
    transpose x1, local copies, waits for them, and re-layouts, on_device(): spread_sum = spread_parts.transpose(0, 2, 3, 1).reshape(cases, 2 * PANELS)  12.1 us
    another operation x1, local copies, waits for them, and re-layouts, on_device(): parts = lax.all_gather(spread_sum, ('col', 'row'), axis=0, tiled=False)  9.83 us
    reduce_sum x1, other arithmetic, on_device(): whole_sum = parts.sum(axis=0)  8.79 us
  transfers between devices with their start and end apart: 1, of which 1 were waited for; matrix products, arithmetic and copies ran while one was open for 0% of the time, Pallas kernels for 0%

profile of v1, /device:TPU:0, one launch (start us, length us, event | category | flops | bytes accessed | tf_op | source)
XLA Modules:
  0.0 266.3 jit_solution(2475848525754027526)
XLA Ops:
  7.2 0.0 all-gather.2.cloned.1.call-start
  7.2 0.7 compare_select_fusion.1
  7.9 0.7 compare_and_fusion.1
  8.6 0.8 gather_fusion
  9.4 0.2 select_bitcast_fusion.1
  9.7 5.7 %slice.13 = bf16[4,128,128]{2,0,1:T(4,128)(2,1)S(1)} slice(bf16[4,128,256]{2,0,1:T(4,128)(2,1)S(1)} %select_bitcast_fusion.1), slice={[0:4:1], [0:128:1], [1:256:2]} | slice | bytes 262144 | tf_op jit(solution)/shard_map/slice | solution.py:10
  15.4 5.7 %slice.12 = bf16[4,128,128]{2,0,1:T(4,128)(2,1)S(1)} slice(bf16[4,128,256]{2,0,1:T(4,128)(2,1)S(1)} %select_bitcast_fusion.1), slice={[0:4:1], [0:128:1], [0:256:2]} | slice | bytes 262144 | tf_op jit(solution)/shard_map/slice | solution.py:10
  21.8 4.4 %fusion.4 = f32[4,2,128,128]{3,0,1,2:T(4,128)S(1)} fusion(bf16[128,128,128]{2,1,0:T(8,128)(2,1)} %param.11, bf16[4,1,128,128]{3,0,1,2:T(4,128)(2,1)S(1)} %bitcast.51, bf16[4,1,128,128]{3,0,1,2:T(4,128)(2,1)S(1)} %bitcast.52), kind=kOutput, calls=%fused_computation.7 | convolution fusion | flops 34078720 | bytes 4980736 | tf_op jit(solution)/shard_map/qpn,ckqn->ckqp/dot_general | solution.py:22
  26.2 1.3 convolution_bitcast_fusion
  27.6 12.1 %copy.15 = f32[4,128,128,2]{0,3,2,1:T(2,128)} copy(f32[4,128,128,2]{1,2,3,0:T(8,128)S(1)} %convolution_bitcast_fusion) | data formatting | bytes 1048576 | tf_op jit(solution)/shard_map/transpose;qb,ckqp->ckbp/transpose | solution.py:32
  39.7 9.8 %copy.16 = f32[1,4,32768]{2,1,0:T(4,128)} copy(f32[1,4,32768]{1,2,0:T(8,128)} %bitcast.48) | data formatting | bytes 1048576 | tf_op jit(solution)/shard_map/all_gather;reshape | solution.py:35
  49.6 117.2 %all-gather.2.cloned.1.call-done = f32[32,4,32768]{2,1,0:T(4,128)} async-done(((f32[1,4,32768]{2,1,0:T(4,128)}), f32[32,4,32768]{2,1,0:T(4,128)}) %all-gather.2.cloned.1.call-update) | async-done | bytes 16777232 | tf_op jit(solution)/shard_map/all_gather | solution.py:35
  166.8 8.8 %reduce_sum.9 = bf16[4,32768]{1,0:T(4,128)(2,1)S(1)} reduce(f32[32,4,32768]{2,1,0:T(4,128)} %all-gather.2.cloned.1.call-done, f32[]{:T(128)} %constant.58.clone.1), dimensions={0}, to_apply=%region_0.1 | reduce | flops 4063232 | bytes 17039364 | tf_op jit(solution)/shard_map/reduce_sum | solution.py:36
  175.6 25.4 %convolution_add_fusion = f32[4,4096]{1,0:T(4,128)S(1)} fusion(bf16[4,8192]{1,0:T(4,128)(2,1)S(1)} %dynamic-slice_convert_fusion, bf16[4096,8192]{1,0:T(8,128)(2,1)} %param.12, s32[]{:T(128)S(6)} %select_n.48, f32[4096]{0:T(1024)S(1)} %copy-done.2, pred[]{:T(512)S(6)} %eq.34), kind=kOutput, calls=%fused_computation.2 | convolution fusion | flops 268500992 | bytes 67289096 | tf_op jit(solution)/shard_map/dot_general | solution.py:45
  201.0 15.9 %psum.7 = bf16[4,4096]{1,0:T(4,128)(2,1)S(1)} all-reduce(f32[4,4096]{1,0:T(4,128)S(1)} %convolution_add_fusion), channel_id=1, replica_groups=mesh['col'=4,'row'=8] {'col'}, use_global_device_ids=true, to_apply=%region_1.2 | all-reduce | flops 16384 | bytes 98304 | tf_op jit(solution)/shard_map/psum | solution.py:49
  217.0 14.4 %all_gather.7 = bf16[4,32768]{1,0:T(4,128)(2,1)S(1)} all-gather(bf16[4,4096]{1,0:T(4,128)(2,1)S(1)} %psum.7), channel_id=1, replica_groups=mesh['col'=4,'row'=8] {'row'}, dimensions={1}, use_global_device_ids=true | all-gather | bytes 294912 | tf_op jit(solution)/shard_map/all_gather | solution.py:50
  231.4 0.8 gather_fusion.1
  232.2 0.2 select_bitcast_fusion
  232.4 5.7 %slice.15 = bf16[4,128,128]{2,0,1:T(4,128)(2,1)S(1)} slice(bf16[4,128,256]{2,0,1:T(4,128)(2,1)S(1)} %select_bitcast_fusion), slice={[0:4:1], [0:128:1], [1:256:2]} | slice | bytes 262144 | tf_op jit(solution)/shard_map/slice | solution.py:10
  238.2 5.7 %slice.14 = bf16[4,128,128]{2,0,1:T(4,128)(2,1)S(1)} slice(bf16[4,128,256]{2,0,1:T(4,128)(2,1)S(1)} %select_bitcast_fusion), slice={[0:4:1], [0:128:1], [0:256:2]} | slice | bytes 262144 | tf_op jit(solution)/shard_map/slice | solution.py:10
  243.9 3.4 %fusion.7 = f32[4,2,128,128]{3,0,1,2:T(4,128)S(1)} fusion(bf16[128,128,128]{2,1,0:T(8,128)(2,1)} %param.11, bf16[4,1,128,128]{3,0,2,1:T(4,128)(2,1)S(1)} %bitcast.53, bf16[4,1,128,128]{3,0,2,1:T(4,128)(2,1)S(1)} %bitcast.54), kind=kOutput, calls=%fused_computation.8 | convolution fusion | flops 33685504 | bytes 4980736 | tf_op jit(solution)/shard_map/qpn,ckqp->ckqn/dot_general | solution.py:53
  247.3 0.4 convolution_bitcast_fusion.1
  247.7 5.9 %copy.22 = f32[4,64,128,2]{0,3,2,1:T(2,128)} copy(f32[4,64,128,2]{2,1,3,0:T(8,128)S(1)} %convolution_bitcast_fusion.1) | data formatting | bytes 524288 | tf_op jit(solution)/shard_map/transpose;qs,ckqn->cksn/transpose | solution.py:61
  253.6 5.9 %copy.23 = f32[4,16384]{1,0:T(4,128)} copy(f32[4,16384]{0,1:T(8,128)} %bitcast.49) | data formatting | bytes 524288
  (17 shorter events, 0.1 us)
Async XLA Ops:
  7.2 1.4 copy-start
  7.2 159.6 %all-gather.2.cloned.1.call-start = ((), (), s32[]{:S(2)}) async-start(), calls=%async_computation | async-start | bytes 17301504 | tf_op jit(solution)/shard_map/all_gather | solution.py:35
  39.6 9.9 %copy-start.3 = (s32[128]{0:T(128)S(1)}, s32[128]{0:T(128)}, u32[]{:S(2)}) copy-start(s32[128]{0:T(128)} %param.9) | copy-start | bytes 1540
  49.6 126.0 %copy-start.2 = (f32[4096]{0:T(1024)S(1)}, f32[4096]{0:T(1024)}, u32[]{:S(2)}) copy-start(f32[4096]{0:T(1024)} %param.13) | copy-start | bytes 49156
  175.6 71.7 %copy-start.4 = (s32[128]{0:T(128)S(1)}, s32[128]{0:T(128)}, u32[]{:S(2)}) copy-start(s32[128]{0:T(128)} %param.8) | copy-start | bytes 1540
  217.0 42.5 %copy-start.1 = (bf16[4,4096]{1,0:T(4,128)(2,1)}, bf16[4,4096]{1,0:T(4,128)(2,1)S(1)}, u32[]{:S(2)}) copy-start(bf16[4,4096]{1,0:T(4,128)(2,1)S(1)} %psum.7) | copy-start | bytes 98308
Sparse Core Ops, SparseCore 0:
  49.6 117.0 all-gather.1
